TPU v7x, 128 devices: a whole 4x4x4 slice. The times are simulated.
128 devices in a mesh: rep: 16 (over x, z), grp: 8 (over y, core).
Axes of the slice: x: 4, y: 4, z: 4, core: 2. Of those that a mesh axis runs over, the one named last changes fastest.
Arguments:
- inputs: bfloat16 [2, 262144, 1152], P(None, ('rep', 'grp')), may hold values from -6 to 6
- out_grads: bfloat16 [2, 262144, 1152], P(None, ('rep', 'grp')), may hold values from -6 to 6
- weights: bfloat16 [2, 1152, 1152], P(None, 'grp'), may hold values from -3 to 3
- biases: bfloat16 [2, 1152], P(None, 'grp'), may hold values from -3 to 3
- errors: float32 [16, 2, 1152, 1152], P('rep', None, 'grp'), may hold values from -6 to 6
- momenta: float32 [2, 1152, 1152], P(None, 'grp'), may hold values from -3 to 3
- bias_momenta: float32 [2, 1152], P(None, 'grp'), may hold values from -3 to 3
- q_start: float32 [2, 1152, 32], replicated, may hold values from -6 to 6
Outputs:
- new_weights: bfloat16 [2, 1152, 1152], replicated
- new_biases: bfloat16 [2, 1152], replicated
- new_errors: float32 [16, 2, 1152, 1152], P('rep', None, 'grp')
- new_momenta: float32 [2, 1152, 1152], P(None, 'grp')
- new_bias_momenta: float32 [2, 1152], P(None, 'grp')
All inputs are finite; a program needn't handle non-finite values.
Results may differ from a plain program's by a relative error of at most 0.0045.
Values may be sent and summed in bfloat16 or wider, within the bound.
No kernel may reach another device: no remote copies, remote signals or barrier semaphores. Data moves between devices by JAX's collectives and lax.ppermute only.
A program may use at most 256 MiB of HBM per device.

v0:
```python
import jax
import jax.numpy as jnp
from jax import lax
from jax.sharding import PartitionSpec as P

ROUNDS = 2
NS_STEPS = 5
HIGH = lax.Precision.HIGHEST


def orthonormal(p_sum, gram):
    fro = jnp.sqrt(jnp.sum(gram * gram, axis=(1, 2))) + 1e-06
    scaled = gram / fro[:, None, None]
    eye = jnp.eye(gram.shape[-1], dtype=jnp.float32)
    ymat = scaled
    zmat = jnp.broadcast_to(eye, gram.shape)
    for step in range(NS_STEPS):
        tmat = 1.5 * eye - 0.5 * jnp.einsum("lab,lbc->lac", zmat, ymat, precision=HIGH)
        ymat = jnp.einsum("lab,lbc->lac", ymat, tmat, precision=HIGH)
        zmat = jnp.einsum("lab,lbc->lac", tmat, zmat, precision=HIGH)
    phat = jnp.einsum("lrk,lkj->lrj", p_sum, zmat, precision=HIGH)
    return phat / jnp.sqrt(fro)[:, None, None]


def body(inputs, out_grads, weights, biases, errors, momenta, bias_momenta, q_start):
    layers = inputs.shape[0]
    tok = inputs.shape[1]
    width = inputs.shape[2]
    groups = lax.axis_size("grp")
    reps = lax.axis_size("rep")
    rows = width // groups
    scale = float(tok) ** (-0.5)
    grads = []
    for layer in range(layers):
        x_layer = inputs[layer]
        y_layer = out_grads[layer]

        def term(start, count, x_layer=x_layer, y_layer=y_layer):
            return jnp.einsum("tr,te->re", x_layer, y_layer, preferred_element_type=jnp.float32)

        grads.append(
            lax.psum_scatter(
                term(jnp.int32(0), lax.axis_size("grp") * rows),
                "grp",
                scatter_dimension=0,
                tiled=True,
            )
        )
    merged = jnp.stack(grads) * scale + errors[0]
    col_sums = jnp.sum(out_grads, axis=1, dtype=jnp.float32)
    bias_total = lax.psum(col_sums, ("rep", "grp")) * (scale / reps)
    bias_rows = biases.shape[1]
    bias_grad = lax.dynamic_slice_in_dim(
        bias_total, lax.axis_index("grp") * bias_rows, bias_rows, 1
    )
    qmat = q_start
    phat = None
    for rnd in range(ROUNDS):
        local_p = jnp.einsum("lre,lek->lrk", merged, qmat, precision=HIGH)
        p_sum = lax.psum(local_p, "rep")
        local_gram = jnp.einsum("lrk,lrj->lkj", p_sum, p_sum, precision=HIGH)
        gram = lax.psum(local_gram, "grp")
        phat = orthonormal(p_sum, gram)
        local_q = jnp.einsum("lre,lrk->lek", merged, phat, precision=HIGH)
        qmat = lax.psum(local_q, ("rep", "grp"))
    approx = jnp.einsum("lrk,lek->lre", phat, qmat, precision=HIGH) / reps
    new_errors = (merged - approx)[None]
    new_momenta = 0.9 * momenta + approx
    weight_shard = (weights.astype(jnp.float32) - 0.5 * new_momenta).astype(jnp.bfloat16)
    new_bias_momenta = 0.9 * bias_momenta + bias_grad
    bias_shard = (biases.astype(jnp.float32) - 0.5 * new_bias_momenta).astype(jnp.bfloat16)
    new_weights, new_biases = (
        lax.all_gather(weight_shard, "grp", axis=1, tiled=True),
        lax.all_gather(bias_shard, "grp", axis=1, tiled=True),
    )
    return (new_weights, new_biases, new_errors, new_momenta, new_bias_momenta)


def solution(mesh):
    placed = (
        P(None, ("rep", "grp"), None),
        P(None, ("rep", "grp"), None),
        P(None, "grp", None),
        P(None, "grp"),
        P("rep", None, "grp", None),
        P(None, "grp", None),
        P(None, "grp"),
        P(),
    )
    return jax.shard_map(
        body,
        mesh=mesh,
        in_specs=placed,
        out_specs=(P(), P(), P("rep", None, "grp", None), P(None, "grp", None), P(None, "grp")),
        check_vma=False,
    )
```

profile of v0, /device:TPU:1, one launch (start us, length us, event | category | flops | bytes accessed | tf_op | source)
XLA Modules:
  0.0 687.0 jit_solution(1677941259270240270)
XLA Ops:
  7.2 12.5 %fusion.3 = f32[1152,1152]{1,0:T(8,128)} fusion(bf16[2,2048,1152]{2,1,0:T(8,128)(2,1)} %param.9, bf16[2,2048,1152]{2,1,0:T(8,128)(2,1)} %param.8), kind=kOutput, calls=%fused_computation.4 | convolution fusion | flops 5435817984 | bytes 14745600 | tf_op jit(solution)/shard_map/tr,te->re/dot_general | solution.py:39
  19.9 12.5 %fusion = f32[1152,1152]{1,0:T(8,128)} fusion(bf16[2,2048,1152]{2,1,0:T(8,128)(2,1)} %param.9, bf16[2,2048,1152]{2,1,0:T(8,128)(2,1)} %param.8), kind=kOutput, calls=%fused_computation.1 | convolution fusion | flops 5435817984 | bytes 14745600 | tf_op jit(solution)/shard_map/tr,te->re/dot_general | solution.py:39
  32.6 28.2 %reduce-scatter.3.cloned.1.call-done = f32[144,1152]{1,0:T(8,128)} async-done(((f32[1152,1152]{1,0:T(8,128)}), f32[144,1152]{1,0:T(8,128)}) %reduce-scatter.3.cloned.1.call-update) | async-done | bytes 663568 | tf_op jit(solution)/shard_map/reduce_scatter | solution.py:42
  60.7 42.6 %reduce-scatter.5.cloned.1.call-done = f32[144,1152]{1,0:T(8,128)} async-done(((f32[1152,1152]{1,0:T(8,128)}), f32[144,1152]{1,0:T(8,128)}) %reduce-scatter.5.cloned.1.call-update) | async-done | bytes 663568 | tf_op jit(solution)/shard_map/reduce_scatter | solution.py:42
  103.3 1.4 fusion.10
  104.8 1.5 fusion.36
  106.3 60.4 %psum.49 = f32[2,144,32]{1,2,0:T(8,128)S(1)} all-reduce(f32[2,144,32]{1,2,0:T(8,128)S(1)} %fusion.36), channel_id=1, replica_groups=mesh['rep'=16,'grp'=8] {'rep'}, use_global_device_ids=true, to_apply=%region_2.0 | all-reduce | flops 9216 | bytes 73728 | tf_op jit(solution)/shard_map/psum | solution.py:60
  166.9 37.5 %psum.50 = f32[2,32,32]{2,1,0:T(8,128)S(1)} all-reduce(f32[2,32,32]{2,1,0:T(8,128)S(1)} %fusion.37), channel_id=1, replica_groups=mesh['rep'=16,'grp'=8] {'grp'}, use_global_device_ids=true, to_apply=%region_3.0 | all-reduce | flops 2048 | bytes 16384 | tf_op jit(solution)/shard_map/psum | solution.py:62
  204.4 0.2 fusion.20
  207.2 1.6 fusion.45
  208.9 139.4 %all-reduce.3.cloned.1.call-done = f32[2,1152,32]{1,2,0:T(8,128)} async-done(((f32[2,1152,32]{1,2,0:T(8,128)}), f32[2,1152,32]{1,2,0:T(8,128)}) %all-reduce.3.cloned.1.call-update) | async-done | bytes 294928 | tf_op jit(solution)/shard_map/psum | solution.py:65
  348.4 2.5 fusion.46
  350.9 58.2 %psum.52 = f32[2,144,32]{1,2,0:T(8,128)S(1)} all-reduce(f32[2,144,32]{1,2,0:T(8,128)S(1)} %fusion.46), channel_id=1, replica_groups=mesh['rep'=16,'grp'=8] {'rep'}, use_global_device_ids=true, to_apply=%region_6.0 | all-reduce | flops 9216 | bytes 73728 | tf_op jit(solution)/shard_map/psum | solution.py:60
  409.3 35.9 %psum.53 = f32[2,32,32]{2,1,0:T(8,128)S(1)} all-reduce(f32[2,32,32]{2,1,0:T(8,128)S(1)} %fusion.47), channel_id=1, replica_groups=mesh['rep'=16,'grp'=8] {'grp'}, use_global_device_ids=true, to_apply=%region_7.0 | all-reduce | flops 2048 | bytes 16384 | tf_op jit(solution)/shard_map/psum | solution.py:62
  445.3 0.2 fusion.15
  448.2 1.6 fusion.55
  449.8 139.4 %all-reduce.5.cloned.1.call-done = f32[2,1152,32]{1,2,0:T(8,128)} async-done(((f32[2,1152,32]{1,2,0:T(8,128)}), f32[2,1152,32]{1,2,0:T(8,128)}) %all-reduce.5.cloned.1.call-update) | async-done | bytes 294928 | tf_op jit(solution)/shard_map/psum | solution.py:65
  589.2 4.4 subtract_convert_fusion
  593.7 5.0 convert_reduce_fusion
  598.7 65.3 %psum.55 = f32[2,1152]{1,0:T(2,128)S(1)} all-reduce(f32[2,1152]{1,0:T(2,128)S(1)} %convert_reduce_fusion), channel_id=1, replica_groups=mesh['rep'=16,'grp'=8] {'rep','grp'}, use_global_device_ids=true, to_apply=%region_11.0 | all-reduce | flops 2304 | bytes 18432 | tf_op jit(solution)/shard_map/psum | solution.py:51
  664.0 0.7 fusion.32
  664.6 9.9 %all-gather = bf16[8,144,2]{1,2,0:T(2,128)(2,1)S(1)} all-gather(bf16[1,144,2]{1,2,0:T(2,128)(2,1)S(1)} %get-tuple-element.5), channel_id=1, replica_groups=mesh['rep'=16,'grp'=8] {'grp'}, dimensions={0}, use_global_device_ids=true | all-gather | bytes 5184 | tf_op jit(solution)/shard_map/all_gather | solution.py:74
  674.5 0.7 reshape.33
  675.2 5.3 copy.22
  (58 shorter events, 6.0 us)
Async XLA Ops:
  7.2 97.6 %copy-start = (f32[2,1152,32]{1,2,0:T(8,128)S(1)}, f32[2,1152,32]{1,2,0:T(8,128)}, u32[]{:S(2)}) copy-start(f32[2,1152,32]{1,2,0:T(8,128)} %param.15) | copy-start | bytes 884740
  7.2 53.5 %reduce-scatter.3.cloned.1.call-start = ((), (), s32[]{:S(2)}) async-start(), calls=%async_computation.2 | async-start | bytes 5971968 | tf_op jit(solution)/shard_map/reduce_scatter | solution.py:42
  19.7 83.6 %reduce-scatter.5.cloned.1.call-start = ((), (), s32[]{:S(2)}) async-start(), calls=%async_computation.3 | async-start | bytes 5971968 | tf_op jit(solution)/shard_map/reduce_scatter | solution.py:42
  32.5 70.8 %copy-start.1 = (f32[1,2,144,1152]{3,2,1,0:T(8,128)S(1)}, f32[1,2,144,1152]{3,2,1,0:T(8,128)}, u32[]{:S(2)}) copy-start(f32[1,2,144,1152]{3,2,1,0:T(8,128)} %param.12) | copy-start | bytes 3981316
  32.5 315.9 %all-reduce.3.cloned.1.call-start = ((), (), s32[]{:S(2)}) async-start(), calls=%async_computation.4 | async-start | bytes 589824 | tf_op jit(solution)/shard_map/psum | solution.py:65
  208.9 380.4 %all-reduce.5.cloned.1.call-start = ((), (), s32[]{:S(2)}) async-start(), calls=%async_computation.5 | async-start | bytes 589824 | tf_op jit(solution)/shard_map/psum | solution.py:65
  447.2 142.1 %copy-start.2 = (f32[2,144,1152]{2,1,0:T(8,128)S(1)}, f32[2,144,1152]{2,1,0:T(8,128)}, u32[]{:S(2)}) copy-start(f32[2,144,1152]{2,1,0:T(8,128)} %param.13) | copy-start | bytes 3981316
  449.8 225.4 %all-gather.3.cloned.1.call-start = ((), (), s32[]{:S(2)}) async-start(), calls=%async_computation.6 | async-start | bytes 5971968 | tf_op jit(solution)/shard_map/all_gather | solution.py:73
  593.7 70.3 %copy-start.3 = (f32[2,144]{1,0:T(2,128)S(1)}, f32[2,144]{1,0:T(2,128)}, u32[]{:S(2)}) copy-start(f32[2,144]{1,0:T(2,128)} %param.14) | copy-start | bytes 3460
  593.7 70.2 %copy-start.4 = (bf16[2,144]{1,0:T(2,128)(2,1)S(1)}, bf16[2,144]{1,0:T(2,128)(2,1)}, u32[]{:S(2)}) copy-start(bf16[2,144]{1,0:T(2,128)(2,1)} %param.11) | copy-start | bytes 1732
Sparse Core Ops, SparseCore 0:
  19.8 40.8 reduce-scatter.2
  63.7 39.5 reduce-scatter.4
  209.0 139.3 all-reduce.2
  449.9 139.3 all-reduce.4
  593.8 36.2 all-gather.2
where the time goes:
time: 687 us
  waiting for transfers between devices  350 us (51%)
  blocking collectives  267 us (39%)
  matrix products  42.4 us (6%)
  between operations  14.1 us (2%)
  other arithmetic  7.32 us (1%)
    psum x2, waiting for transfers between devices, body(): qmat = lax.psum(local_q, ('rep', 'grp'))  279 us
    psum x2, blocking collectives, body(): p_sum = lax.psum(local_p, 'rep')  119 us
    psum x2, blocking collectives, body(): gram = lax.psum(local_gram, 'grp')  73.4 us
    reduce_scatter x2, waiting for transfers between devices, body(): lax.psum_scatter(term(jnp.int32(0), lax.axis_size('grp') * rows), 'grp',...  70.7 us
    psum x1, blocking collectives, body(): bias_total = lax.psum(col_sums, ('rep', 'grp')) * (scale / reps)  65.3 us
    dot_general x2, matrix products, term(): jnp.einsum('tr,te->re', x_layer, y_layer, preferred_element_type=jnp.floa...  25 us
  transfers between devices with their start and end apart: 5, of which 4 were waited for; matrix products, arithmetic and copies ran while one was open for 3% of the time, Pallas kernels for 0%

commit v1 on v0

--- a/solution.py
+++ b/solution.py
@@ -1,3 +1,4 @@
+import functools
 import jax
 import jax.numpy as jnp
 from jax import lax
@@ -6,6 +7,17 @@
 ROUNDS = 2
 NS_STEPS = 5
 HIGH = lax.Precision.HIGHEST
+
+
+def assign_ranges(s0, axis_id):
+    k_all = lax.axis_size(axis_id)
+    later = s0
+    for k0 in [[(ii, ii ^ j0) for ii in range(k_all)] for j0 in (1, 2, 4, 8, 16) if j0 < k_all]:
+        later = later + lax.ppermute(later, axis_name=axis_id, perm=k0)
+    return later
+
+
+compute_ways_here = functools.partial(assign_ranges, axis_id="rep")
 
 
 def orthonormal(p_sum, gram):
@@ -57,7 +69,7 @@
     phat = None
     for rnd in range(ROUNDS):
         local_p = jnp.einsum("lre,lek->lrk", merged, qmat, precision=HIGH)
-        p_sum = lax.psum(local_p, "rep")
+        p_sum = compute_ways_here(local_p)
         local_gram = jnp.einsum("lrk,lrj->lkj", p_sum, p_sum, precision=HIGH)
         gram = lax.psum(local_gram, "grp")
         phat = orthonormal(p_sum, gram)

time: 687 us -> 591 us (0.86)
  blocking collectives: 267 us -> 130 us
  waiting for transfers between devices: 350 us -> 375 us
  starting transfers between devices: 0.39 us -> 15.3 us
    psum x2 -> x0, blocking collectives: 119 us -> none  [body(): p_sum = lax.psum(local_p, 'rep')]
    psum x2, blocking collectives: 73.4 us -> 54.6 us  [body(): gram = lax.psum(local_gram, 'grp')]
    ppermute x0 -> x8, waiting for transfers between devices: none -> 16.8 us  [assign_ranges(): later = later + lax.ppermute(later, axis_name=axis_id, perm=k0)]
    ppermute x0 -> x8, starting transfers between devices: none -> 14.7 us  [assign_ranges(): later = later + lax.ppermute(later, axis_name=axis_id, perm=k0)]
    psum x2, waiting for transfers between devices: 279 us -> 288 us  [body(): qmat = lax.psum(local_q, ('rep', 'grp'))]
  transfers between devices with their start and end apart: 5 -> 13, of which waited for: 4 -> 12; matrix products, arithmetic and copies ran while one was open for 3% -> 3% of each run, Pallas kernels for 0% -> 0%
where the time goes in v1:
time: 591 us; the launch traced here: 590 us
  waiting for transfers between devices  375 us (63%)
  blocking collectives  130 us (22%)
  matrix products  42.4 us (7%)
  starting transfers between devices  15.3 us (3%)
  between operations  14.1 us (2%)
  other arithmetic  7.39 us (1%)
  local copies, waits for them, and re-layouts  6.02 us (1%)
    psum x2, waiting for transfers between devices, body(): qmat = lax.psum(local_q, ('rep', 'grp'))  288 us
    reduce_scatter x2, waiting for transfers between devices, body(): lax.psum_scatter(term(jnp.int32(0), lax.axis_size('grp') * rows), 'grp',...  70.8 us
    psum x1, blocking collectives, body(): bias_total = lax.psum(col_sums, ('rep', 'grp')) * (scale / reps)  65.2 us
    psum x2, blocking collectives, body(): gram = lax.psum(local_gram, 'grp')  54.6 us
    dot_general x2, matrix products, term(): jnp.einsum('tr,te->re', x_layer, y_layer, preferred_element_type=jnp.floa...  25 us
    ppermute x8, waiting for transfers between devices, assign_ranges(): later = later + lax.ppermute(later, axis_name=axis_id, perm=k0)  16.8 us
    ppermute x8, starting transfers between devices, assign_ranges(): later = later + lax.ppermute(later, axis_name=axis_id, perm=k0)  14.7 us
  transfers between devices with their start and end apart: 13, of which 12 were waited for; matrix products, arithmetic and copies ran while one was open for 3% of the time, Pallas kernels for 0%

profile of v1, /device:TPU:1, one launch (start us, length us, event | category | flops | bytes accessed | tf_op | source)
XLA Modules:
  0.0 590.3 jit_solution(1055742230637638989)
XLA Ops:
  7.2 12.5 %fusion.3 = f32[1152,1152]{1,0:T(8,128)} fusion(bf16[2,2048,1152]{2,1,0:T(8,128)(2,1)} %param.9, bf16[2,2048,1152]{2,1,0:T(8,128)(2,1)} %param.8), kind=kOutput, calls=%fused_computation.4 | convolution fusion | flops 5435817984 | bytes 14745600 | tf_op jit(solution)/shard_map/tr,te->re/dot_general | solution.py:51
  20.0 12.5 %fusion = f32[1152,1152]{1,0:T(8,128)} fusion(bf16[2,2048,1152]{2,1,0:T(8,128)(2,1)} %param.9, bf16[2,2048,1152]{2,1,0:T(8,128)(2,1)} %param.8), kind=kOutput, calls=%fused_computation.1 | convolution fusion | flops 5435817984 | bytes 14745600 | tf_op jit(solution)/shard_map/tr,te->re/dot_general | solution.py:51
  32.5 28.2 %reduce-scatter.3.cloned.1.call-done = f32[144,1152]{1,0:T(8,128)} async-done(((f32[1152,1152]{1,0:T(8,128)}), f32[144,1152]{1,0:T(8,128)}) %reduce-scatter.3.cloned.1.call-update) | async-done | bytes 663568 | tf_op jit(solution)/shard_map/reduce_scatter | solution.py:54
  60.7 42.6 %reduce-scatter.5.cloned.1.call-done = f32[144,1152]{1,0:T(8,128)} async-done(((f32[1152,1152]{1,0:T(8,128)}), f32[144,1152]{1,0:T(8,128)}) %reduce-scatter.5.cloned.1.call-update) | async-done | bytes 663568 | tf_op jit(solution)/shard_map/reduce_scatter | solution.py:54
  109.5 2.9 collective-permute-start.1
  115.5 1.9 collective-permute-done.2
  117.4 2.7 collective-permute-start.3
  120.2 1.9 collective-permute-done.3
  122.3 28.2 %psum.35 = f32[2,32,32]{2,1,0:T(8,128)S(1)} all-reduce(f32[2,32,32]{2,1,0:T(8,128)S(1)} %fusion.37), channel_id=1, replica_groups=mesh['rep'=16,'grp'=8] {'grp'}, use_global_device_ids=true, to_apply=%region_2.0 | all-reduce | flops 2048 | bytes 16384 | tf_op jit(solution)/shard_map/psum | solution.py:74
  155.3 145.1 %all-reduce.3.cloned.1.call-done = f32[2,1152,32]{1,2,0:T(8,128)} async-done(((f32[2,1152,32]{1,2,0:T(8,128)}), f32[2,1152,32]{1,2,0:T(8,128)}) %all-reduce.3.cloned.1.call-update) | async-done | bytes 294928 | tf_op jit(solution)/shard_map/psum | solution.py:77
  300.4 2.5 fusion.46
  304.1 2.0 collective-permute-done.4
  306.1 2.3 collective-permute-start.5
  308.4 2.4 collective-permute-done.5
  311.6 2.5 collective-permute-done.6
  314.1 2.3 collective-permute-start.7
  316.3 2.4 collective-permute-done.7
  319.0 26.4 %psum.37 = f32[2,32,32]{2,1,0:T(8,128)S(1)} all-reduce(f32[2,32,32]{2,1,0:T(8,128)S(1)} %fusion.47), channel_id=1, replica_groups=mesh['rep'=16,'grp'=8] {'grp'}, use_global_device_ids=true, to_apply=%region_5.0 | all-reduce | flops 2048 | bytes 16384 | tf_op jit(solution)/shard_map/psum | solution.py:74
  350.0 142.6 %all-reduce.5.cloned.1.call-done = f32[2,1152,32]{1,2,0:T(8,128)} async-done(((f32[2,1152,32]{1,2,0:T(8,128)}), f32[2,1152,32]{1,2,0:T(8,128)}) %all-reduce.5.cloned.1.call-update) | async-done | bytes 294928 | tf_op jit(solution)/shard_map/psum | solution.py:77
  492.6 4.4 subtract_convert_fusion
  497.0 5.0 convert_reduce_fusion
  502.0 65.2 %psum.39 = f32[2,1152]{1,0:T(2,128)S(1)} all-reduce(f32[2,1152]{1,0:T(2,128)S(1)} %convert_reduce_fusion), channel_id=1, replica_groups=mesh['rep'=16,'grp'=8] {'rep','grp'}, use_global_device_ids=true, to_apply=%region_9.0 | all-reduce | flops 2304 | bytes 18432 | tf_op jit(solution)/shard_map/psum | solution.py:63
  567.9 9.9 %all-gather = bf16[8,144,2]{1,2,0:T(2,128)(2,1)S(1)} all-gather(bf16[1,144,2]{1,2,0:T(2,128)(2,1)S(1)} %get-tuple-element.5), channel_id=1, replica_groups=mesh['rep'=16,'grp'=8] {'grp'}, dimensions={0}, use_global_device_ids=true | all-gather | bytes 5184 | tf_op jit(solution)/shard_map/all_gather | solution.py:86
  578.5 5.3 copy.22
  (80 shorter events, 22.4 us)
Async XLA Ops:
  7.2 97.6 %copy-start = (f32[2,1152,32]{1,2,0:T(8,128)S(1)}, f32[2,1152,32]{1,2,0:T(8,128)}, u32[]{:S(2)}) copy-start(f32[2,1152,32]{1,2,0:T(8,128)} %param.15) | copy-start | bytes 884740
  7.2 53.6 %reduce-scatter.3.cloned.1.call-start = ((), (), s32[]{:S(2)}) async-start(), calls=%async_computation.2 | async-start | bytes 5971968 | tf_op jit(solution)/shard_map/reduce_scatter | solution.py:54
  19.7 83.6 %reduce-scatter.5.cloned.1.call-start = ((), (), s32[]{:S(2)}) async-start(), calls=%async_computation.3 | async-start | bytes 5971968 | tf_op jit(solution)/shard_map/reduce_scatter | solution.py:54
  32.5 70.8 %copy-start.1 = (f32[1,2,144,1152]{3,2,1,0:T(8,128)S(1)}, f32[1,2,144,1152]{3,2,1,0:T(8,128)}, u32[]{:S(2)}) copy-start(f32[1,2,144,1152]{3,2,1,0:T(8,128)} %param.12) | copy-start | bytes 3981316
  32.5 267.9 %all-reduce.3.cloned.1.call-start = ((), (), s32[]{:S(2)}) async-start(), calls=%async_computation.4 | async-start | bytes 589824 | tf_op jit(solution)/shard_map/psum | solution.py:77
  106.3 3.2 collective-permute-start
  109.5 4.7 collective-permute-start.1
  114.2 3.2 collective-permute-start.2
  117.4 4.7 collective-permute-start.3
  155.0 337.5 %all-reduce.5.cloned.1.call-start = ((), (), s32[]{:S(2)}) async-start(), calls=%async_computation.5 | async-start | bytes 589824 | tf_op jit(solution)/shard_map/psum | solution.py:77
  302.9 3.2 collective-permute-start.4
  306.1 4.7 collective-permute-start.5
  310.8 3.2 collective-permute-start.6
  314.1 4.7 collective-permute-start.7
  347.4 145.2 %copy-start.2 = (f32[2,144,1152]{2,1,0:T(8,128)S(1)}, f32[2,144,1152]{2,1,0:T(8,128)}, u32[]{:S(2)}) copy-start(f32[2,144,1152]{2,1,0:T(8,128)} %param.13) | copy-start | bytes 3981316
  349.9 228.6 %all-gather.3.cloned.1.call-start = ((), (), s32[]{:S(2)}) async-start(), calls=%async_computation.6 | async-start | bytes 5971968 | tf_op jit(solution)/shard_map/all_gather | solution.py:85
  497.0 70.2 %copy-start.3 = (f32[2,144]{1,0:T(2,128)S(1)}, f32[2,144]{1,0:T(2,128)}, u32[]{:S(2)}) copy-start(f32[2,144]{1,0:T(2,128)} %param.14) | copy-start | bytes 3460
  497.0 70.2 %copy-start.4 = (bf16[2,144]{1,0:T(2,128)(2,1)S(1)}, bf16[2,144]{1,0:T(2,128)(2,1)}, u32[]{:S(2)}) copy-start(bf16[2,144]{1,0:T(2,128)(2,1)} %param.11) | copy-start | bytes 1732
Sparse Core Ops, SparseCore 0:
  19.9 40.8 reduce-scatter.2
  63.7 39.5 reduce-scatter.4
  155.1 145.2 all-reduce.2
  350.1 142.4 all-reduce.4
  497.1 36.2 all-gather.2
